TPU v7x, 32 devices: a whole 2x2x4 slice. The times are simulated.
32 devices in a mesh: win: 16 (over z, y, x), strip: 2 (over core).
Axes of the slice: x: 2, y: 2, z: 4, core: 2. Of those that a mesh axis runs over, the one named last changes fastest.
Arguments:
- start_states: float32 [16, 3, 32, 1024], P('win', None, 'strip'), may hold values from -1.5 to 1.5
- obs_cells: int32 [16, 4, 512], P('win', None, 'strip'), may hold values from 0 to 16383
- obs_values: float32 [16, 4, 512], P('win', None, 'strip'), may hold values from -1.5 to 1.5
- weighting: float32 [3, 128, 128], replicated, may hold values from -0.5 to 0.5
- live_windows: int32 [16], P('win'), may hold values 0 or 1
Outputs:
- gradient: float32 [16, 3, 32, 1024], P('win', None, 'strip')
- analysis: float32 [16, 3, 32, 1024], P('win', None, 'strip')
Inputs may be any that keep to these rules, and one draw needn't show every extreme that they name: `obs_cells`: each entry indexes a cell of its own row strip as (row within the strip) * 1024 + column.
All inputs are finite; a program needn't handle non-finite values. No bound on the sum of `live_windows` on one device may be relied on, other than what follows from the above.
Results may differ from a plain program's by a relative error of at most 0.0003.
Values sent between devices are 32-bit elements; how exact they have to be, the bound alone decides.
A program may use at most 64 MiB of HBM per device.

v0:
```python
import jax
import jax.numpy as jnp
from jax import lax
from jax.sharding import PartitionSpec as P

TIME_STEP = 0.2
DIFFUSION = 0.12
CORIOLIS = 0.5
STEP_LENGTH = 0.5


def extended(shard, sides, width):
    for axis, dim in sides:
        devices, length = (lax.axis_size(axis), shard.shape[dim])
        up = [(i, (i + 1) % devices) for i in range(devices - 1)]
        down = [(j, i) for i, j in up]
        last = lax.slice_in_dim(shard, length - width, length, axis=dim)
        leading = lax.slice_in_dim(shard, 0, width, axis=dim)
        before = lax.ppermute(last, axis, up)
        after = lax.ppermute(leading, axis, down)
        shard = jnp.concatenate([before, shard, after], axis=dim)
    return shard


def from_behind(shard, axis, by):
    devices = lax.axis_size(axis)
    pairs = [(i, i + by) for i in range(devices) if 0 <= i + by < devices]
    return lax.ppermute(shard, axis, pairs)


def col_diff(field):
    return (jnp.roll(field[1:-1], -1, 1) - jnp.roll(field[1:-1], 1, 1)) * 0.5


def row_diff(field):
    return (field[2:] - field[:-2]) * 0.5


def laplace(field):
    inner = field[1:-1]
    return field[2:] + field[:-2] + jnp.roll(inner, -1, 1) + jnp.roll(inner, 1, 1) - 4.0 * inner


def advance(padded):
    height, east_wind, north_wind = (padded[0], padded[1], padded[2])
    depth = 1.0 + height
    flux_east = east_wind * depth
    flux_north = north_wind * depth
    height_in, east_in, north_in = (height[1:-1], east_wind[1:-1], north_wind[1:-1])
    new_height = (
        height_in
        - TIME_STEP * (col_diff(flux_east) + row_diff(flux_north))
        + DIFFUSION * laplace(height)
    )
    new_east = (
        east_in
        - TIME_STEP
        * (col_diff(height) + east_in * col_diff(east_wind) + north_in * row_diff(east_wind))
        + TIME_STEP * CORIOLIS * north_in
        + DIFFUSION * laplace(east_wind)
    )
    new_north = (
        north_in
        - TIME_STEP
        * (row_diff(height) + east_in * col_diff(north_wind) + north_in * row_diff(north_wind))
        - TIME_STEP * CORIOLIS * east_in
        + DIFFUSION * laplace(north_wind)
    )
    return jnp.stack([new_height, new_east, new_north])


def weigh(defect, weighting):
    fields, rows, cols = defect.shape
    width = weighting.shape[1]
    blocks = defect.reshape(fields, rows, cols // width, width)
    mixed = jnp.einsum("frbi,fij->frbj", blocks, weighting, precision=lax.Precision.HIGHEST)
    return defect + mixed.reshape(fields, rows, cols)


def forcing(adjoint, state, cells, values, alive, read_rows, write_rows):
    cols = state.shape[2]
    source = state[0].reshape(state.shape[1] * cols)
    innovation = (source[cells + read_rows * cols] - values) * alive
    target = adjoint[0].reshape(adjoint.shape[1] * cols)
    target = target.at[cells + write_rows * cols].add(innovation)
    return adjoint.at[0].set(target.reshape(adjoint.shape[1], cols))


def inside_map(field, strip_base, total_rows, margin):
    rows_here = field.shape[1]
    row_ids = strip_base - margin + jnp.arange(rows_here)
    inside = (row_ids >= 0) & (row_ids < total_rows)
    return jnp.where(inside[None, :, None], field, 0.0)


def per_device(start_states, obs_cells, obs_values, weighting, live_windows):
    state = start_states[0]
    cells = obs_cells[0]
    values = obs_values[0]
    rows = state.shape[1]
    steps = cells.shape[0]
    strip_base = lax.axis_index("strip") * rows
    total_rows = rows * lax.axis_size("strip")
    alive = live_windows[0].astype(state.dtype)
    trajectory = []
    wide = extended(state, (("strip", 1),), steps)
    for moment in range(steps):
        trajectory.append(wide)
        wide = advance(wide)
        margin = steps - moment - 1
        if margin > 0:
            wide = inside_map(wide, strip_base, total_rows, margin)
    previous_end = from_behind(wide, "win", 1)
    own_weighted = weigh(state - previous_end, weighting)
    next_weighted = from_behind(own_weighted, "win", -1)
    adjoint = forcing(-next_weighted, wide, cells[steps - 1], values[steps - 1], alive, 0, 0)
    for moment in range(steps - 1, -1, -1):
        unused, pullback = jax.vjp(advance, trajectory[moment])
        adjoint = pullback(adjoint)[0]
        margin = steps - moment
        adjoint = inside_map(adjoint, strip_base, total_rows, margin)
        if moment > 0:
            adjoint = forcing(
                adjoint,
                trajectory[moment],
                cells[moment - 1],
                values[moment - 1],
                alive,
                margin,
                margin,
            )
    spill = jnp.concatenate([adjoint[:, :steps], adjoint[:, steps + rows :]], axis=1)
    received = extended(spill, (("strip", 1),), steps)
    owned = adjoint[:, steps : steps + rows]
    owned = owned.at[:, :steps].add(received[:, :steps])
    owned = owned.at[:, rows - steps :].add(received[:, 3 * steps :])
    adjoint = owned
    gradient = own_weighted + adjoint
    analysis = state - STEP_LENGTH * gradient
    return (gradient[None], analysis[None])


def solution(mesh):
    placed = (
        P("win", None, "strip", None),
        P("win", None, "strip"),
        P("win", None, "strip"),
        P(),
        P("win"),
    )
    return jax.shard_map(
        per_device,
        mesh=mesh,
        in_specs=placed,
        out_specs=(P("win", None, "strip", None), P("win", None, "strip", None)),
        check_vma=False,
    )
```

profile of v0, /device:TPU:7, one launch (start us, length us, event | category | flops | bytes accessed | tf_op | source)
XLA Modules:
  0.0 88.2 jit_solution(5338380200915076691)
XLA Ops:
  0.7 1.0 %fusion.156 = (f32[3,4,1024]{2,1,0:T(4,128)S(1)}, f32[3,4,1024]{2,1,0:T(4,128)S(1)}) fusion(f32[3,16,1024]{2,1,0:T(8,128)} %bitcast.596), kind=kLoop, calls=%fused_computation.442 | loop fusion | bytes 196608 | tf_op jit(solution)/shard_map/slice | solution.py:17
  1.7 1.3 %collective-permute-start = (f32[3,4,1024]{2,1,0:T(4,128)S(1)}, f32[3,4,1024]{2,1,0:T(4,128)S(1)}, u32[]{:S(2)}, u32[]{:S(2)}) collective-permute-start(f32[3,4,1024]{2,1,0:T(4,128)S(1)} %get-tuple-element.230), channel_id=1, source_target_pairs={{0,1},{2,3},{4,5},{6,7},{8,9},{10,11},{12,13},{14,15},{16,17},{18,... | collective-permute-start | bytes 147464 | tf_op jit(solution)/shard_map/ppermute | solution.py:19
  3.0 3.0 %collective-permute-start.1 = (f32[3,4,1024]{2,1,0:T(4,128)S(1)}, f32[3,4,1024]{2,1,0:T(4,128)S(1)}, u32[]{:S(2)}, u32[]{:S(2)}) collective-permute-start(f32[3,4,1024]{2,1,0:T(4,128)S(1)} %get-tuple-element.231), channel_id=1, source_target_pairs={{1,0},{3,2},{5,4},{7,6},{9,8},{11,10},{13,12},{15,14},{17,16},{19,... | collective-permute-start | bytes 147464 | tf_op jit(solution)/shard_map/ppermute | solution.py:20
  6.8 0.7 copy-done.46
  9.0 0.7 fusion.161
  9.9 0.7 fusion.163
  11.6 0.7 fusion.172
  12.3 0.7 fusion.171
  13.2 0.7 fusion.174
  13.9 0.7 fusion.173
  15.4 0.7 fusion.182
  16.1 0.7 fusion.181
  16.9 0.7 fusion.184
  17.7 0.7 fusion.183
  19.1 0.7 fusion.206
  20.0 0.7 fusion.208
  21.1 3.3 %collective-permute-start.2 = (f32[3,16,1024]{2,1,0:T(8,128)S(1)}, f32[3,16,1024]{2,1,0:T(8,128)S(1)}, u32[]{:S(2)}, u32[]{:S(2)}) collective-permute-start(f32[3,16,1024]{2,1,0:T(8,128)S(1)} %pad_maximum_fusion.1), channel_id=1, source_target_pairs={{0,2},{2,4},{4,6},{6,8},{8,10},{10,12},{12,14},{14,16},{16,18},{18... | collective-permute-start | bytes 589832 | tf_op jit(solution)/shard_map/ppermute | solution.py:28
  24.4 0.9 slice-done.1
  25.3 0.9 slice-done
  26.2 1.7 %gather_fusion = f32[256]{0:T(256)S(1)} fusion(f32[16384]{0:T(1024)S(1)} %bitcast.595, s32[1024]{0:T(1024)S(1)} %pad_clamp_fusion.3), kind=kCustom, calls=%fused_computation | custom fusion | bytes 3072 | tf_op jit(solution)/shard_map/gather | solution.py:83
  27.9 1.7 %gather_fusion.1 = f32[256]{0:T(256)S(1)} fusion(f32[18432]{0:T(1024)S(1)} %reshape_squeeze.23, s32[1024]{0:T(1024)S(1)} %pad_clamp_fusion.2), kind=kCustom, calls=%fused_computation.1 | custom fusion | bytes 3072 | tf_op jit(solution)/shard_map/gather | solution.py:83
  30.2 1.7 %gather_fusion.2 = f32[256]{0:T(256)S(1)} fusion(f32[20480]{0:T(1024)S(1)} %reshape_squeeze.25, s32[1024]{0:T(1024)S(1)} %pad_clamp_fusion.1), kind=kCustom, calls=%fused_computation.2 | custom fusion | bytes 3072 | tf_op jit(solution)/shard_map/gather | solution.py:83
  32.0 1.7 %gather_fusion.3 = f32[256]{0:T(256)S(1)} fusion(f32[22528]{0:T(1024)S(1)} %reshape_squeeze.27, s32[1024]{0:T(1024)S(1)} %pad_clamp_fusion), kind=kCustom, calls=%fused_computation.3 | custom fusion | bytes 3072 | tf_op jit(solution)/shard_map/gather | solution.py:83
  34.8 2.3 %collective-permute-start.3 = (f32[3,16,1024]{2,1,0:T(8,128)S(1)}, f32[3,16,1024]{2,1,0:T(8,128)S(1)}, u32[]{:S(2)}, u32[]{:S(2)}) collective-permute-start(f32[3,16,1024]{2,1,0:T(8,128)S(1)} %add.1055), channel_id=1, source_target_pairs={{2,0},{4,2},{6,4},{8,6},{10,8},{12,10},{14,12},{16,14},{18,16},{20... | collective-permute-start | bytes 589832 | tf_op jit(solution)/shard_map/ppermute | solution.py:28
  37.7 7.7 %collective-permute-done.3 = f32[3,16,1024]{2,1,0:T(8,128)S(1)} collective-permute-done((f32[3,16,1024]{2,1,0:T(8,128)S(1)}, f32[3,16,1024]{2,1,0:T(8,128)S(1)}, u32[]{:S(2)}, u32[]{:S(2)}) %collective-permute-start.3) | collective-permute-done | bytes 196640 | tf_op jit(solution)/shard_map/ppermute | solution.py:28
  46.0 2.0 %scatter_fusion = f32[16384]{0:T(1024)S(1)} fusion(f32[16384]{0:T(1024)S(1)} %bitcast.594, s32[256]{0:T(256)S(1)} %bitcast.625, f32[256]{0:T(256)S(1)} %subtract_multiply_fusion.11), kind=kCustom, calls=%fused_computation.4 | custom fusion | flops 256 | bytes 4096 | tf_op jit(solution)/shard_map/scatter-add | solution.py:85
  49.9 0.7 copy-done.16
  51.5 0.9 copy-done.4
  53.5 0.7 fusion.180
  54.2 2.1 %scatter_fusion.1 = f32[18432]{0:T(1024)S(1)} fusion(f32[18432]{0:T(1024)S(1)} %reshape_squeeze.22, s32[256]{0:T(256)} %bitcast.623, f32[256]{0:T(256)} %subtract_multiply_fusion.10), kind=kCustom, calls=%fused_computation.5 | custom fusion | flops 256 | bytes 4096 | tf_op jit(solution)/shard_map/scatter-add | solution.py:85
  56.8 0.7 copy-done.21
  58.1 0.6 copy-done.26
  59.7 0.7 copy-done.12
  61.4 0.9 copy-done.2
  63.4 0.7 fusion.170
  64.7 2.3 %scatter_fusion.2 = f32[20480]{0:T(1024)S(1)} fusion(f32[20480]{0:T(1024)S(1)} %reshape_squeeze.24, s32[256]{0:T(256)S(1)} %bitcast.621, f32[256]{0:T(256)} %subtract_multiply_fusion.9), kind=kCustom, calls=%fused_computation.6 | custom fusion | flops 256 | bytes 4096 | tf_op jit(solution)/shard_map/scatter-add | solution.py:85
  67.6 0.7 copy-done.23
  68.8 0.6 copy-done.27
  70.4 0.7 copy-done.8
  73.1 0.7 fusion.158
  73.8 0.7 fusion.160
  74.6 0.6 copy-done.44
  75.2 2.0 %scatter_fusion.3 = f32[22528]{0:T(1024)S(1)} fusion(f32[22528]{0:T(1024)S(1)} %reshape_squeeze.26, s32[256]{0:T(256)S(1)} %bitcast.619, f32[256]{0:T(256)S(1)} %copy-done.44), kind=kCustom, calls=%fused_computation.7 | custom fusion | flops 256 | bytes 4096 | tf_op jit(solution)/shard_map/scatter-add | solution.py:85
  77.7 0.7 copy-done.24
  82.2 1.3 %collective-permute-start.4 = (f32[3,4,1024]{2,1,0:T(4,128)S(1)}, f32[3,4,1024]{2,1,0:T(4,128)S(1)}, u32[]{:S(2)}, u32[]{:S(2)}) collective-permute-start(f32[3,4,1024]{2,1,0:T(4,128)S(1)} %get-tuple-element.137), channel_id=1, source_target_pairs={{0,1},{2,3},{4,5},{6,7},{8,9},{10,11},{12,13},{14,15},{16,17},{18,... | collective-permute-start | bytes 147464 | tf_op jit(solution)/shard_map/ppermute | solution.py:19
  83.5 3.0 %collective-permute-start.5 = (f32[3,4,1024]{2,1,0:T(4,128)S(1)}, f32[3,4,1024]{2,1,0:T(4,128)S(1)}, u32[]{:S(2)}, u32[]{:S(2)}) collective-permute-start(f32[3,4,1024]{2,1,0:T(4,128)S(1)} %get-tuple-element.136), channel_id=1, source_target_pairs={{1,0},{3,2},{5,4},{7,6},{9,8},{11,10},{13,12},{15,14},{17,16},{19,... | collective-permute-start | bytes 147464 | tf_op jit(solution)/shard_map/ppermute | solution.py:20
  86.6 0.8 collective-permute-done.5
  87.5 0.8 subtract_bitcast_fusion
  (323 shorter events, 24.3 us)
Async XLA Ops:
  0.6 33.8 %copy-start = (f32[3,128,128]{2,1,0:T(8,128)S(1)}, f32[3,128,128]{2,1,0:T(8,128)}, u32[]{:S(2)}) copy-start(f32[3,128,128]{2,1,0:T(8,128)} %param.20) | copy-start | bytes 589828
  0.6 8.1 %copy-start.7 = (f32[1,3,16,1024]{3,2,1,0:T(8,128)S(1)}, f32[1,3,16,1024]{3,2,1,0:T(8,128)}, u32[]{:S(2)}) copy-start(f32[1,3,16,1024]{3,2,1,0:T(8,128)} %param.17) | copy-start | bytes 589828
  1.7 7.1 %collective-permute-start = (f32[3,4,1024]{2,1,0:T(4,128)S(1)}, f32[3,4,1024]{2,1,0:T(4,128)S(1)}, u32[]{:S(2)}, u32[]{:S(2)}) collective-permute-start(f32[3,4,1024]{2,1,0:T(4,128)S(1)} %get-tuple-element.230), channel_id=1, source_target_pairs={{0,1},{2,3},{4,5},{6,7},{8,9},{10,11},{12,13},{14,15},{16,17},{18,... | collective-permute-start | bytes 147464 | tf_op jit(solution)/shard_map/ppermute | solution.py:19
  3.0 5.8 %collective-permute-start.1 = (f32[3,4,1024]{2,1,0:T(4,128)S(1)}, f32[3,4,1024]{2,1,0:T(4,128)S(1)}, u32[]{:S(2)}, u32[]{:S(2)}) collective-permute-start(f32[3,4,1024]{2,1,0:T(4,128)S(1)} %get-tuple-element.231), channel_id=1, source_target_pairs={{1,0},{3,2},{5,4},{7,6},{9,8},{11,10},{13,12},{15,14},{17,16},{19,... | collective-permute-start | bytes 147464 | tf_op jit(solution)/shard_map/ppermute | solution.py:20
  6.0 5.0 %copy-start.47 = (pred[22]{0:T(512)(128)(4,1)}, pred[22]{0:T(512)(128)(4,1)S(1)}, u32[]{:S(2)}) copy-start(pred[22]{0:T(512)(128)(4,1)S(1)} %compare_and_fusion.1) | copy-start | bytes 70
  6.1 8.8 %copy-start.49 = (pred[20]{0:T(512)(128)(4,1)}, pred[20]{0:T(512)(128)(4,1)S(1)}, u32[]{:S(2)}) copy-start(pred[20]{0:T(512)(128)(4,1)S(1)} %compare_and_fusion.2) | copy-start | bytes 64
  6.7 11.9 %copy-start.51 = (pred[18]{0:T(512)(128)(4,1)}, pred[18]{0:T(512)(128)(4,1)S(1)}, u32[]{:S(2)}) copy-start(pred[18]{0:T(512)(128)(4,1)S(1)} %compare_and_fusion.3) | copy-start | bytes 58
  6.8 0.7 copy-start.43
  6.8 0.7 copy-start.41
  11.2 9.6 %copy-start.1 = (f32[3,22,1024]{2,1,0:T(8,128)}, f32[3,22,1024]{2,1,0:T(8,128)S(1)}, u32[]{:S(2)}) copy-start(f32[3,22,1024]{2,1,0:T(8,128)S(1)} %maximum_select_fusion) | copy-start | bytes 811012
  14.9 5.9 %copy-start.3 = (f32[3,20,1024]{2,1,0:T(8,128)}, f32[3,20,1024]{2,1,0:T(8,128)S(1)}, u32[]{:S(2)}) copy-start(f32[3,20,1024]{2,1,0:T(8,128)S(1)} %maximum_select_fusion.1) | copy-start | bytes 737284
  18.7 2.2 %copy-start.5 = (f32[3,18,1024]{2,1,0:T(8,128)}, f32[3,18,1024]{2,1,0:T(8,128)S(1)}, u32[]{:S(2)}) copy-start(f32[3,18,1024]{2,1,0:T(8,128)S(1)} %maximum_select_fusion.2) | copy-start | bytes 663556
  21.1 3.3 %slice-start.2 = ((f32[3,18,1024]{2,1,0:T(8,128)}), f32[1,18,1024]{2,1,0:T(8,128)S(1)}, s32[]{:S(2)}) async-start(f32[3,18,1024]{2,1,0:T(8,128)} %copy-done.5), calls=%async_computation.2 | async-start | bytes 196608 | tf_op jit(solution)/shard_map/slice | solution.py:45
  21.1 13.2 %collective-permute-start.2 = (f32[3,16,1024]{2,1,0:T(8,128)S(1)}, f32[3,16,1024]{2,1,0:T(8,128)S(1)}, u32[]{:S(2)}, u32[]{:S(2)}) collective-permute-start(f32[3,16,1024]{2,1,0:T(8,128)S(1)} %pad_maximum_fusion.1), channel_id=1, source_target_pairs={{0,2},{2,4},{4,6},{6,8},{8,10},{10,12},{12,14},{14,16},{16,18},{18... | collective-permute-start | bytes 589832 | tf_op jit(solution)/shard_map/ppermute | solution.py:28
  24.4 0.9 %slice-start.1 = ((f32[3,20,1024]{2,1,0:T(8,128)}), f32[1,20,1024]{2,1,0:T(8,128)S(1)}, s32[]{:S(2)}) async-start(f32[3,20,1024]{2,1,0:T(8,128)} %copy-done.3), calls=%async_computation.1 | async-start | bytes 196608 | tf_op jit(solution)/shard_map/slice | solution.py:45
  25.3 0.9 %slice-start = ((f32[3,22,1024]{2,1,0:T(8,128)}), f32[1,22,1024]{2,1,0:T(8,128)S(1)}, s32[]{:S(2)}) async-start(f32[3,22,1024]{2,1,0:T(8,128)} %copy-done.1), calls=%async_computation | async-start | bytes 196608 | tf_op jit(solution)/shard_map/slice | solution.py:45
  34.8 10.7 %copy-start.6 = (f32[3,18,1024]{2,1,0:T(8,128)S(1)}, f32[3,18,1024]{2,1,0:T(8,128)}, u32[]{:S(2)}) copy-start(f32[3,18,1024]{2,1,0:T(8,128)} %copy-done.5) | copy-start | bytes 663556
  34.8 10.6 %collective-permute-start.3 = (f32[3,16,1024]{2,1,0:T(8,128)S(1)}, f32[3,16,1024]{2,1,0:T(8,128)S(1)}, u32[]{:S(2)}, u32[]{:S(2)}) collective-permute-start(f32[3,16,1024]{2,1,0:T(8,128)S(1)} %add.1055), channel_id=1, source_target_pairs={{2,0},{4,2},{6,4},{8,6},{10,8},{12,10},{14,12},{16,14},{18,16},{20... | collective-permute-start | bytes 589832 | tf_op jit(solution)/shard_map/ppermute | solution.py:28
  49.7 0.8 copy-start.16
  49.8 0.9 copy-start.17
  49.8 0.9 %copy-start.18 = (f32[16,1023]{1,0:T(8,128)S(1)}, f32[16,1023]{1,0:T(8,128)}, u32[]{:S(2)}) copy-start(f32[16,1023]{1,0:T(8,128)} %get-tuple-element.385) | copy-start | bytes 196420
  49.8 0.9 %copy-start.19 = (f32[16,1023]{1,0:T(8,128)S(1)}, f32[16,1023]{1,0:T(8,128)}, u32[]{:S(2)}) copy-start(f32[16,1023]{1,0:T(8,128)} %get-tuple-element.388) | copy-start | bytes 196420
  51.4 1.0 %copy-start.4 = (f32[3,20,1024]{2,1,0:T(8,128)S(1)}, f32[3,20,1024]{2,1,0:T(8,128)}, u32[]{:S(2)}) copy-start(f32[3,20,1024]{2,1,0:T(8,128)} %copy-done.3) | copy-start | bytes 737284
  59.5 0.9 %copy-start.12 = (f32[18,1023]{1,0:T(8,128)S(1)}, f32[18,1023]{1,0:T(8,128)}, u32[]{:S(2)}) copy-start(f32[18,1023]{1,0:T(8,128)} %get-tuple-element.306) | copy-start | bytes 220972
  59.5 0.9 %copy-start.13 = (f32[18,1023]{1,0:T(8,128)S(1)}, f32[18,1023]{1,0:T(8,128)}, u32[]{:S(2)}) copy-start(f32[18,1023]{1,0:T(8,128)} %get-tuple-element.309) | copy-start | bytes 220972
  59.5 1.0 %copy-start.14 = (f32[18,1023]{1,0:T(8,128)S(1)}, f32[18,1023]{1,0:T(8,128)}, u32[]{:S(2)}) copy-start(f32[18,1023]{1,0:T(8,128)} %get-tuple-element.314) | copy-start | bytes 220972
  59.5 1.0 %copy-start.15 = (f32[18,1023]{1,0:T(8,128)S(1)}, f32[18,1023]{1,0:T(8,128)}, u32[]{:S(2)}) copy-start(f32[18,1023]{1,0:T(8,128)} %get-tuple-element.317) | copy-start | bytes 220972
  59.5 1.0 %copy-start.38 = (f32[18,1]{1,0:T(8,128)S(1)}, f32[18,1]{1,0:T(8,128)}, u32[]{:S(2)}) copy-start(f32[18,1]{1,0:T(8,128)} %get-tuple-element.305) | copy-start | bytes 220
  59.5 1.0 %copy-start.39 = (f32[18,1]{1,0:T(8,128)S(1)}, f32[18,1]{1,0:T(8,128)}, u32[]{:S(2)}) copy-start(f32[18,1]{1,0:T(8,128)} %get-tuple-element.310) | copy-start | bytes 220
  59.6 1.0 %copy-start.40 = (f32[18,1]{1,0:T(8,128)S(1)}, f32[18,1]{1,0:T(8,128)}, u32[]{:S(2)}) copy-start(f32[18,1]{1,0:T(8,128)} %get-tuple-element.313) | copy-start | bytes 220
  59.7 0.8 copy-start.37
  61.3 1.0 %copy-start.2 = (f32[3,22,1024]{2,1,0:T(8,128)S(1)}, f32[3,22,1024]{2,1,0:T(8,128)}, u32[]{:S(2)}) copy-start(f32[3,22,1024]{2,1,0:T(8,128)} %copy-done.1) | copy-start | bytes 811012
  67.5 0.7 copy-start.23
  70.2 0.9 %copy-start.8 = (f32[20,1023]{1,0:T(8,128)S(1)}, f32[20,1023]{1,0:T(8,128)}, u32[]{:S(2)}) copy-start(f32[20,1023]{1,0:T(8,128)} %get-tuple-element.275) | copy-start | bytes 245524
  70.2 0.9 %copy-start.9 = (f32[20,1023]{1,0:T(8,128)S(1)}, f32[20,1023]{1,0:T(8,128)}, u32[]{:S(2)}) copy-start(f32[20,1023]{1,0:T(8,128)} %get-tuple-element.278) | copy-start | bytes 245524
  70.2 1.0 %copy-start.10 = (f32[20,1023]{1,0:T(8,128)S(1)}, f32[20,1023]{1,0:T(8,128)}, u32[]{:S(2)}) copy-start(f32[20,1023]{1,0:T(8,128)} %get-tuple-element.283) | copy-start | bytes 245524
  70.2 1.0 %copy-start.11 = (f32[20,1023]{1,0:T(8,128)S(1)}, f32[20,1023]{1,0:T(8,128)}, u32[]{:S(2)}) copy-start(f32[20,1023]{1,0:T(8,128)} %get-tuple-element.286) | copy-start | bytes 245524
  70.3 1.0 %copy-start.34 = (f32[20,1]{1,0:T(8,128)S(1)}, f32[20,1]{1,0:T(8,128)}, u32[]{:S(2)}) copy-start(f32[20,1]{1,0:T(8,128)} %get-tuple-element.274) | copy-start | bytes 244
  70.3 1.0 %copy-start.35 = (f32[20,1]{1,0:T(8,128)S(1)}, f32[20,1]{1,0:T(8,128)}, u32[]{:S(2)}) copy-start(f32[20,1]{1,0:T(8,128)} %get-tuple-element.279) | copy-start | bytes 244
  70.3 1.0 %copy-start.36 = (f32[20,1]{1,0:T(8,128)S(1)}, f32[20,1]{1,0:T(8,128)}, u32[]{:S(2)}) copy-start(f32[20,1]{1,0:T(8,128)} %get-tuple-element.282) | copy-start | bytes 244
  70.4 0.8 copy-start.33
  77.7 0.7 copy-start.24
  77.7 0.7 copy-start.25
  77.7 0.7 copy-start.20
  80.4 0.7 copy-start.31
  80.4 0.7 copy-start.32
  82.2 4.4 %collective-permute-start.4 = (f32[3,4,1024]{2,1,0:T(4,128)S(1)}, f32[3,4,1024]{2,1,0:T(4,128)S(1)}, u32[]{:S(2)}, u32[]{:S(2)}) collective-permute-start(f32[3,4,1024]{2,1,0:T(4,128)S(1)} %get-tuple-element.137), channel_id=1, source_target_pairs={{0,1},{2,3},{4,5},{6,7},{8,9},{10,11},{12,13},{14,15},{16,17},{18,... | collective-permute-start | bytes 147464 | tf_op jit(solution)/shard_map/ppermute | solution.py:19
  83.5 3.9 %collective-permute-start.5 = (f32[3,4,1024]{2,1,0:T(4,128)S(1)}, f32[3,4,1024]{2,1,0:T(4,128)S(1)}, u32[]{:S(2)}, u32[]{:S(2)}) collective-permute-start(f32[3,4,1024]{2,1,0:T(4,128)S(1)} %get-tuple-element.136), channel_id=1, source_target_pairs={{1,0},{3,2},{5,4},{7,6},{9,8},{11,10},{13,12},{15,14},{17,16},{19,... | collective-permute-start | bytes 147464 | tf_op jit(solution)/shard_map/ppermute | solution.py:20
  (15 other events, 10.2 us)
where the time goes:
time: 89.5 us; the launch traced here: 88.2 us
  local copies, waits for them, and re-layouts  42.3 us (47%)
  other arithmetic  19.9 us (22%)
  starting transfers between devices  14.2 us (16%)
  waiting for transfers between devices  8.55 us (10%)
  between operations  2.9 us (3%)
    unnamed x112, local copies, waits for them, and re-layouts  13.7 us
    slice x24, local copies, waits for them, and re-layouts, col_diff(): return (jnp.roll(field[1:-1], -1, 1) - jnp.roll(field[1:-1], 1, 1)) * 0.5  9.45 us
    scatter-add x4, other arithmetic, forcing(): target = target.at[cells + write_rows * cols].add(innovation)  8.36 us
    ppermute x2, waiting for transfers between devices, from_behind(): return lax.ppermute(shard, axis, pairs)  7.72 us
    gather x4, local copies, waits for them, and re-layouts, forcing(): innovation = (source[cells + read_rows * cols] - values) * alive  6.89 us
    ppermute x2, starting transfers between devices, extended(): after = lax.ppermute(leading, axis, down)  6.06 us
    ppermute x2, starting transfers between devices, from_behind(): return lax.ppermute(shard, axis, pairs)  5.55 us
    split x48, local copies, waits for them, and re-layouts, col_diff(): return (jnp.roll(field[1:-1], -1, 1) - jnp.roll(field[1:-1], 1, 1)) * 0.5  4.32 us
  transfers between devices with their start and end apart: 6, of which 2 were waited for; matrix products, arithmetic and copies ran while one was open for 11% of the time, Pallas kernels for 0%

commit v1 on v0

v1 whole, which is shorter than its diff:
```python
import functools

import jax
import jax.numpy as jnp
from jax import lax
from jax.experimental import pallas as pl
from jax.experimental.pallas import tpu as pltpu
from jax.sharding import PartitionSpec as P

TIME_STEP = 0.2
DIFFUSION = 0.12
CORIOLIS = 0.5
STEP_LENGTH = 0.5
LANES = 128
SUBS = 8
CHUNK = 2


def next_col(x, last_lane):
    turned = pltpu.roll(x, LANES - 1, 2)
    return jnp.where(last_lane, pltpu.roll(turned, SUBS - 1, 1), turned)


def prev_col(x, first_lane):
    turned = pltpu.roll(x, 1, 2)
    return jnp.where(first_lane, pltpu.roll(turned, 1, 1), turned)


def kernel(
    n_win, n_strip,
    start_hbm, cells_hbm, values_hbm, weight_hbm, live_hbm,
    grad_hbm, ana_hbm,
    own, above, below, nxt, prev_end, cells, values, weight, live,
    rhs, traj, saved, end, lam, counts, sums, nw, spill_up, spill_down, got_top, got_bot,
    grad, ana,
    local_sem, out_sem, send_sem, recv_sem,
):
    fields, rows, cols = own.shape
    steps = cells.shape[0]
    span = rows + 2 * steps
    pad = 1
    win, strip = lax.axis_index("win"), lax.axis_index("strip")
    has_prev, has_next = win > 0, win < n_win - 1
    has_up, has_down = strip > 0, strip < n_strip - 1

    def at_win(by):
        return {"win": jnp.clip(win + by, 0, n_win - 1)}

    def at_strip(by):
        return {"strip": jnp.clip(strip + by, 0, n_strip - 1)}

    loads = [
        pltpu.make_async_copy(start_hbm.at[0], own, local_sem.at[0]),
        pltpu.make_async_copy(cells_hbm.at[0], cells, local_sem.at[1]),
        pltpu.make_async_copy(values_hbm.at[0], values, local_sem.at[2]),
        pltpu.make_async_copy(weight_hbm, weight, local_sem.at[3]),
        pltpu.make_async_copy(live_hbm, live, local_sem.at[4]),
    ]
    for load in loads:
        load.start()

    barrier = pltpu.get_barrier_semaphore()
    for there, peer in ((has_up, at_strip(-1)), (has_down, at_strip(1)), (has_prev, at_win(-1)), (has_next, at_win(1))):
        @pl.when(there)
        def _():
            pl.semaphore_signal(barrier, inc=1, device_id=peer, device_id_type=pl.DeviceIdType.MESH)
    pl.semaphore_wait(barrier, sum(there.astype(jnp.int32) for there in (has_up, has_down, has_prev, has_next)))

    def remote(src, dst, sem, peer):
        return pltpu.make_async_remote_copy(
            src_ref=src, dst_ref=dst, send_sem=send_sem.at[sem], recv_sem=recv_sem.at[sem],
            device_id=peer, device_id_type=pl.DeviceIdType.MESH,
        )

    halo_up = remote(start_hbm.at[0, :, 0:SUBS, :], below, 0, at_strip(-1))
    halo_down = remote(start_hbm.at[0, :, rows - SUBS:rows, :], above, 1, at_strip(1))
    start_back = [remote(start_hbm.at[0, f], nxt.at[f], 2 + f, at_win(-1)) for f in range(fields)]
    end_on = remote(end, prev_end, 5, at_win(1))
    spill_to_up = remote(spill_up, got_bot, 6, at_strip(-1))
    spill_to_down = remote(spill_down, got_top, 7, at_strip(1))

    @pl.when(has_up)
    def _():
        halo_up.start()

    @pl.when(has_down)
    def _():
        halo_down.start()

    @pl.when(has_prev)
    def _():
        for copy in start_back:
            copy.start()

    lane = lax.broadcasted_iota(jnp.int32, (1, SUBS, LANES), 2)
    first_lane, last_lane = lane == 0, lane == LANES - 1
    zero_row = jnp.zeros((SUBS, LANES), jnp.float32)

    for buf in range(2):
        for f in range(fields):
            for row in list(range(0, steps + pad)) + list(range(steps + pad + rows, span + 2 * pad)):
                lam[buf, f, SUBS * row:SUBS * (row + 1), :] = zero_row
    for j in range(steps):
        for row in (j - 1 + pad, span - j + pad):
            for f in range(fields):
                traj[j, f, SUBS * row:SUBS * (row + 1), :] = zero_row
        for row in (j + pad, span - j - 1 + pad):
            for f in range(fields):
                saved[j, f, SUBS * row:SUBS * (row + 1), :] = zero_row

    loads[0].wait()
    for f in range(fields):
        for g in range(0, rows, SUBS):
            for b in range(SUBS):
                base = SUBS * (steps + pad + g) + b
                traj[0, f, pl.ds(base, SUBS, stride=SUBS), :] = own[f, g:g + SUBS, b * LANES:(b + 1) * LANES]

    loads[1].wait()
    loads[2].wait()
    loads[4].wait()
    alive = live[0].astype(jnp.float32)
    n_obs = cells.shape[1]
    tiles = rows * SUBS
    tile_id = lax.broadcasted_iota(jnp.int32, (tiles, n_obs), 0)
    lane_id = lax.broadcasted_iota(jnp.int32, (LANES, n_obs), 0)
    for j in range(steps):
        cell = cells[j:j + 1, :]
        value = values[j:j + 1, :]
        in_tile = tile_id == lax.shift_right_logical(cell, 7)
        in_lane = lane_id == (cell & (LANES - 1))
        high = value.astype(jnp.bfloat16).astype(jnp.float32)
        low = value - high
        picks = jnp.concatenate(
            [
                jnp.where(in_tile, 1.0, 0.0).astype(jnp.bfloat16),
                jnp.where(in_tile, high, 0.0).astype(jnp.bfloat16),
                jnp.where(in_tile, low, 0.0).astype(jnp.bfloat16),
            ],
            axis=0,
        )
        dense = lax.dot_general(
            picks, jnp.where(in_lane, 1.0, 0.0).astype(jnp.bfloat16),
            (((1,), (1,)), ((), ())), preferred_element_type=jnp.float32,
        )
        counts[j] = alive * dense[:tiles]
        sums[j] = alive * (dense[tiles:2 * tiles] + dense[2 * tiles:])

    loads[3].wait()
    for f in range(fields):
        w = weight[f]
        w_high = w.astype(jnp.bfloat16)
        w_low = (w - w_high.astype(jnp.float32)).astype(jnp.bfloat16)
        rhs[f, 0:LANES, 0:LANES] = w_high
        rhs[f, 0:LANES, LANES:] = w_low
        rhs[f, LANES:, 0:LANES] = w_high
        rhs[f, LANES:, LANES:] = jnp.zeros_like(w_low)

    def weigh(f, defect):
        high = defect.astype(jnp.bfloat16)
        low = (defect - high.astype(jnp.float32)).astype(jnp.bfloat16)
        out = jnp.dot(jnp.concatenate([high, low], axis=1), rhs[f], preferred_element_type=jnp.float32)
        return defect + (out[:, :LANES] + out[:, LANES:])

    for there, copy, src, src_row, dst_row in (
        (has_up, halo_down, above, SUBS - steps, pad),
        (has_down, halo_up, below, 0, pad + steps + rows),
    ):
        @pl.when(there)
        def _():
            copy.wait_recv()
            for f in range(fields):
                for b in range(SUBS):
                    base = SUBS * dst_row + b
                    traj[0, f, pl.ds(base, steps, stride=SUBS), :] = src[f, src_row:src_row + steps, b * LANES:(b + 1) * LANES]

        @pl.when(jnp.logical_not(there))
        def _():
            for f in range(fields):
                traj[0, f, SUBS * dst_row:SUBS * (dst_row + steps), :] = jnp.zeros((SUBS * steps, LANES), jnp.float32)

    up_mask = jnp.where(has_up, 1.0, 0.0).astype(jnp.float32)
    down_mask = jnp.where(has_down, 1.0, 0.0).astype(jnp.float32)

    def pieces(lo, hi):
        edges = []
        for a, b, mask in ((lo, min(hi, steps), up_mask), (steps + rows, hi, down_mask), (steps, steps + rows, None)):
            for r in range(a, b, CHUNK):
                edges.append((r, min(r + CHUNK, b), mask))
        return edges

    def tiles_of(ref, index, lo, hi):
        return ref[index + (slice(SUBS * (lo + pad), SUBS * (hi + pad)), slice(None))].reshape(hi - lo, SUBS, LANES)

    def put(ref, index, lo, value):
        count = value.shape[0]
        ref[index + (slice(SUBS * (lo + pad), SUBS * (lo + count + pad)), slice(None))] = value.reshape(count * SUBS, LANES)

    half = 0.5 * TIME_STEP
    turn = TIME_STEP * CORIOLIS

    for j in range(steps):
        for lo, hi, mask in pieces(j + 1, span - j - 1):
            h = tiles_of(traj, (j, 0), lo - 1, hi + 1)
            e = tiles_of(traj, (j, 1), lo - 1, hi + 1)
            n = tiles_of(traj, (j, 2), lo - 1, hi + 1)
            h0, e0, n0 = h[1:-1], e[1:-1], n[1:-1]
            hr, er, nr = (next_col(x, last_lane) for x in (h0, e0, n0))
            hl, el, nl = (prev_col(x, first_lane) for x in (h0, e0, n0))
            n_dx = nr - nl
            put(saved, (j, 0), lo, el)
            put(saved, (j, 1), lo, er)
            put(saved, (j, 2), lo, n_dx)
            flux_n = n * h + n
            he = h0 * (1.0 - 4.0 * DIFFUSION) - half * ((er * hr + er) - (el * hl + el) + flux_n[2:] - flux_n[:-2]) + DIFFUSION * (hr + hl + h[2:] + h[:-2])
            ee = e0 * (1.0 - 4.0 * DIFFUSION) - half * ((hr - hl) + e0 * (er - el) + n0 * (e[2:] - e[:-2])) + turn * n0 + DIFFUSION * (er + el + e[2:] + e[:-2])
            ne = n0 * (1.0 - 4.0 * DIFFUSION) - half * ((h[2:] - h[:-2]) + e0 * n_dx + n0 * (n[2:] - n[:-2])) - turn * e0 + DIFFUSION * (nr + nl + n[2:] + n[:-2])
            for f, x in enumerate((he, ee, ne)):
                if mask is not None:
                    x = x * mask
                if j + 1 < steps:
                    put(traj, (j + 1, f), lo, x)
                else:
                    put(end, (f,), lo - steps - pad, x)

    @pl.when(has_next)
    def _():
        end_on.start()

    for f in range(fields):
        @pl.when(has_next)
        def _():
            start_back[f].wait_recv()
            for g in range(0, rows, SUBS):
                for b in range(SUBS):
                    nw[f, pl.ds(SUBS * g + b, SUBS, stride=SUBS), :] = nxt[f, g:g + SUBS, b * LANES:(b + 1) * LANES]
            nw[f] = weigh(f, nw[f] - end[f])

        @pl.when(jnp.logical_not(has_next))
        def _():
            nw[f] = jnp.zeros((tiles, LANES), jnp.float32)

    own_rows = slice(SUBS * (steps + pad), SUBS * (steps + rows + pad))
    for f in range(fields):
        force = -nw[f]
        if f == 0:
            force = force + (counts[steps - 1] * end[0] - sums[steps - 1])
        lam[0, f, own_rows, :] = force

    for j in range(steps - 1, -1, -1):
        now = (steps - 1 - j) % 2
        later = 1 - now
        for lo, hi, mask in pieces(j, span - j):
            p, q, r = (tiles_of(lam, (now, f), lo - 1, hi + 1) for f in range(3))
            h0 = tiles_of(traj, (j, 0), lo, hi)
            e = tiles_of(traj, (j, 1), lo - 1, hi + 1)
            n = tiles_of(traj, (j, 2), lo - 1, hi + 1)
            el = tiles_of(saved, (j, 0), lo, hi)
            er = tiles_of(saved, (j, 1), lo, hi)
            n_dx = tiles_of(saved, (j, 2), lo, hi)
            e0, n0 = e[1:-1], n[1:-1]
            p0, q0, r0 = p[1:-1], q[1:-1], r[1:-1]
            pr, qr, rr = (next_col(x, last_lane) for x in (p0, q0, r0))
            pl_, ql, rl = (prev_col(x, first_lane) for x in (p0, q0, r0))
            dxp, dyp = pr - pl_, p[2:] - p[:-2]
            qn, rn = q * n, r * n
            ah = p0 * (1.0 - 4.0 * DIFFUSION) + half * (e0 * dxp + n0 * dyp + (qr - ql) + (r[2:] - r[:-2])) + DIFFUSION * (pr + pl_ + p[2:] + p[:-2])
            ae = q0 * (1.0 - 4.0 * DIFFUSION) + half * ((h0 * dxp + dxp) - q0 * (er - el) + (qr * er - ql * el) + (qn[2:] - qn[:-2]) - r0 * n_dx) - turn * r0 + DIFFUSION * (qr + ql + q[2:] + q[:-2])
            an = r0 * (1.0 - 4.0 * DIFFUSION) + half * ((h0 * dyp + dyp) - q0 * (e[2:] - e[:-2]) - r0 * (n[2:] - n[:-2]) + (rr * er - rl * el) + (rn[2:] - rn[:-2])) + turn * q0 + DIFFUSION * (rr + rl + r[2:] + r[:-2])
            if j > 0 and mask is None:
                at = slice(SUBS * (lo - steps), SUBS * (hi - steps))
                shape = (hi - lo, SUBS, LANES)
                ah = ah + (counts[j - 1, at, :].reshape(shape) * h0 - sums[j - 1, at, :].reshape(shape))
            for f, x in enumerate((ah, ae, an)):
                if mask is not None:
                    x = x * mask
                if j == 0 and lo < steps:
                    spill_up[f, SUBS * lo:SUBS * hi, :] = x.reshape((hi - lo) * SUBS, LANES)
                elif j == 0 and lo >= steps + rows:
                    at = slice(SUBS * (lo - steps - rows), SUBS * (hi - steps - rows))
                    spill_down[f, at, :] = x.reshape((hi - lo) * SUBS, LANES)
                else:
                    put(lam, (later, f), lo, x)
            if j == 0 and hi == span:
                @pl.when(has_up)
                def _():
                    spill_to_up.start()

                @pl.when(has_down)
                def _():
                    spill_to_down.start()

    last = steps % 2

    @pl.when(has_prev)
    def _():
        end_on.wait_recv()

    @pl.when(jnp.logical_not(has_prev))
    def _():
        prev_end[...] = jnp.zeros_like(prev_end)

    for f in range(fields):
        start = traj[0, f, own_rows, :]
        lam[last, f, own_rows, :] = lam[last, f, own_rows, :] + weigh(f, start - prev_end[f])

    @pl.when(has_up)
    def _():
        spill_to_down.wait_recv()
        for f in range(fields):
            at = slice(SUBS * (steps + pad), SUBS * (2 * steps + pad))
            lam[last, f, at, :] = lam[last, f, at, :] + got_top[f]

    @pl.when(has_down)
    def _():
        spill_to_up.wait_recv()
        for f in range(fields):
            at = slice(SUBS * (rows + pad), SUBS * (steps + rows + pad))
            lam[last, f, at, :] = lam[last, f, at, :] + got_bot[f]

    for f in range(fields):
        for g in range(0, rows, SUBS):
            for b in range(SUBS):
                at = pl.ds(SUBS * (steps + pad + g) + b, SUBS, stride=SUBS)
                value = lam[last, f, at, :]
                where = (f, slice(g, g + SUBS), slice(b * LANES, (b + 1) * LANES))
                grad[where] = value
                ana[where] = own[where] - STEP_LENGTH * value

    out = [
        pltpu.make_async_copy(grad, grad_hbm.at[0], out_sem.at[0]),
        pltpu.make_async_copy(ana, ana_hbm.at[0], out_sem.at[1]),
    ]
    for copy in out:
        copy.start()
    for there, copies in (
        (has_up, [halo_up, spill_to_up]),
        (has_down, [halo_down, spill_to_down]),
        (has_prev, start_back),
        (has_next, [end_on]),
    ):
        @pl.when(there)
        def _():
            for copy in copies:
                copy.wait_send()
    for copy in out:
        copy.wait()


def per_device(start_states, obs_cells, obs_values, weighting, live_windows):
    n_win, n_strip = lax.axis_size("win"), lax.axis_size("strip")
    _, fields, rows, cols = start_states.shape
    steps, n_obs = obs_cells.shape[1:]
    span = rows + 2 * steps + 2
    f32 = jnp.float32
    hbm = pl.BlockSpec(memory_space=pl.ANY)
    out = jax.ShapeDtypeStruct(start_states.shape, f32)
    dma = pltpu.SemaphoreType.DMA
    return pl.pallas_call(
        functools.partial(kernel, n_win, n_strip),
        out_shape=(out, out),
        in_specs=[hbm] * 5,
        out_specs=(hbm, hbm),
        scratch_shapes=[
            pltpu.VMEM((fields, rows, cols), f32),
            pltpu.VMEM((fields, SUBS, cols), f32),
            pltpu.VMEM((fields, SUBS, cols), f32),
            pltpu.VMEM((fields, rows, cols), f32),
            pltpu.VMEM((fields, rows * SUBS, LANES), f32),
            pltpu.VMEM((steps, n_obs), jnp.int32),
            pltpu.VMEM((steps, n_obs), f32),
            pltpu.VMEM(weighting.shape, f32),
            pltpu.SMEM((1,), jnp.int32),
            pltpu.VMEM((fields, 2 * LANES, 2 * LANES), jnp.bfloat16),
            pltpu.VMEM((steps, fields, span * SUBS, LANES), f32),
            pltpu.VMEM((steps, fields, span * SUBS, LANES), f32),
            pltpu.VMEM((fields, rows * SUBS, LANES), f32),
            pltpu.VMEM((2, fields, span * SUBS, LANES), f32),
            pltpu.VMEM((steps, rows * SUBS, LANES), f32),
            pltpu.VMEM((steps, rows * SUBS, LANES), f32),
            pltpu.VMEM((fields, rows * SUBS, LANES), f32),
            pltpu.VMEM((fields, steps * SUBS, LANES), f32),
            pltpu.VMEM((fields, steps * SUBS, LANES), f32),
            pltpu.VMEM((fields, steps * SUBS, LANES), f32),
            pltpu.VMEM((fields, steps * SUBS, LANES), f32),
            pltpu.VMEM((fields, rows, cols), f32),
            pltpu.VMEM((fields, rows, cols), f32),
            dma((5,)),
            dma((2,)),
            dma((8,)),
            dma((8,)),
        ],
        compiler_params=pltpu.CompilerParams(collective_id=0, has_side_effects=True),
    )(start_states, obs_cells, obs_values, weighting, live_windows)


def solution(mesh):
    placed = (
        P("win", None, "strip", None),
        P("win", None, "strip"),
        P("win", None, "strip"),
        P(),
        P("win"),
    )
    return jax.shard_map(
        per_device,
        mesh=mesh,
        in_specs=placed,
        out_specs=(P("win", None, "strip", None), P("win", None, "strip", None)),
        check_vma=False,
    )
```

time: 89.5 us -> 19.2 us (0.21)
  the two profiles are of different devices: /device:TPU:7 before, /device:TPU:21 now
where the time goes in v1:
time: 19.2 us; the launch traced here: 19.1 us
  Pallas kernels  15.4 us (80%)
  local copies, waits for them, and re-layouts  2.34 us (12%)
  between operations  1.29 us (7%)
    pallas_call x1, Pallas kernels, per_device(): pl.pallas_call(functools.partial(kernel, n_win, n_strip), out_shape=(out,...  15.4 us
    unnamed x4, local copies, waits for them, and re-layouts  2.34 us

profile of v1, /device:TPU:21, one launch (start us, length us, event | category | flops | bytes accessed | tf_op | source)
XLA Modules:
  0.0 19.1 jit_solution(3657261527332759080)
XLA Ops:
  1.3 15.4 %shard_map.68 = (f32[1,3,16,1024]{3,2,1,0:T(8,128)}, f32[1,3,16,1024]{3,2,1,0:T(8,128)}) custom-call(f32[1,3,16,1024]{3,2,1,0:T(8,128)} %start_hbm.1, s32[1,4,256]{2,1,0:T(4,128)} %cells_hbm.1, f32[1,4,256]{2,1,0:T(4,128)} %values_hbm.1, f32[3,128,128]{2,1,0:T(8,128)} %weight_hbm.1, s32[1]{0:T(128)S(6)} %copy.9.live_hbm), custom_call_target="tpu_custom_call" | custom-call | tf_op jit(solution)/shard_map/pallas_call | solution.py:358
  16.7 0.0 copy-start
  16.7 1.7 %copy.10 = f32[1,3,16,1024]{3,2,1,0:T(8,128)} copy(f32[1,3,16,1024]{3,2,1,0:T(8,128)} %get-tuple-element.4) | data formatting | bytes 393216
  18.4 0.0 copy-done
  18.4 0.7 %copy.11 = f32[1,3,16,1024]{3,2,1,0:T(8,128)} copy(f32[1,3,16,1024]{3,2,1,0:T(8,128)S(1)} %copy-done) | data formatting | bytes 393216
Async XLA Ops:
  16.7 1.7 %copy-start = (f32[1,3,16,1024]{3,2,1,0:T(8,128)S(1)}, f32[1,3,16,1024]{3,2,1,0:T(8,128)}, u32[]{:S(2)}) copy-start(f32[1,3,16,1024]{3,2,1,0:T(8,128)} %get-tuple-element.5) | copy-start | bytes 589828

commit v2 on v1

--- a/solution.py
+++ b/solution.py
@@ -29,11 +29,10 @@
 def kernel(
     n_win, n_strip,
     start_hbm, cells_hbm, values_hbm, weight_hbm, live_hbm,
-    grad_hbm, ana_hbm,
+    grad,
     own, above, below, nxt, prev_end, cells, values, weight, live,
     rhs, traj, saved, end, lam, counts, sums, nw, spill_up, spill_down, got_top, got_bot,
-    grad, ana,
-    local_sem, out_sem, send_sem, recv_sem,
+    local_sem, send_sem, recv_sem,
 ):
     fields, rows, cols = own.shape
     steps = cells.shape[0]
@@ -301,37 +300,22 @@
 
     for f in range(fields):
         start = traj[0, f, own_rows, :]
-        lam[last, f, own_rows, :] = lam[last, f, own_rows, :] + weigh(f, start - prev_end[f])
+        grad[f] = lam[last, f, own_rows, :] + weigh(f, start - prev_end[f])
 
     @pl.when(has_up)
     def _():
         spill_to_down.wait_recv()
         for f in range(fields):
-            at = slice(SUBS * (steps + pad), SUBS * (2 * steps + pad))
-            lam[last, f, at, :] = lam[last, f, at, :] + got_top[f]
+            at = slice(0, SUBS * steps)
+            grad[f, at, :] = grad[f, at, :] + got_top[f]
 
     @pl.when(has_down)
     def _():
         spill_to_up.wait_recv()
         for f in range(fields):
-            at = slice(SUBS * (rows + pad), SUBS * (steps + rows + pad))
-            lam[last, f, at, :] = lam[last, f, at, :] + got_bot[f]
-
-    for f in range(fields):
-        for g in range(0, rows, SUBS):
-            for b in range(SUBS):
-                at = pl.ds(SUBS * (steps + pad + g) + b, SUBS, stride=SUBS)
-                value = lam[last, f, at, :]
-                where = (f, slice(g, g + SUBS), slice(b * LANES, (b + 1) * LANES))
-                grad[where] = value
-                ana[where] = own[where] - STEP_LENGTH * value
-
-    out = [
-        pltpu.make_async_copy(grad, grad_hbm.at[0], out_sem.at[0]),
-        pltpu.make_async_copy(ana, ana_hbm.at[0], out_sem.at[1]),
-    ]
-    for copy in out:
-        copy.start()
+            at = slice(SUBS * (rows - steps), SUBS * rows)
+            grad[f, at, :] = grad[f, at, :] + got_bot[f]
+
     for there, copies in (
         (has_up, [halo_up, spill_to_up]),
         (has_down, [halo_down, spill_to_down]),
@@ -342,6 +326,25 @@
         def _():
             for copy in copies:
                 copy.wait_send()
+
+
+def finish(tiled, start_hbm, grad_hbm, ana_hbm, own, grad, ana, sems):
+    fields, rows, _ = own.shape
+    load = pltpu.make_async_copy(start_hbm.at[0], own, sems.at[0])
+    load.start()
+    load.wait()
+    out = []
+    for f in range(fields):
+        for g in range(0, rows, SUBS):
+            for b in range(SUBS):
+                value = tiled[f, pl.ds(SUBS * g + b, SUBS, stride=SUBS), :]
+                where = (f, slice(g, g + SUBS), slice(b * LANES, (b + 1) * LANES))
+                grad[where] = value
+                ana[where] = own[where] - STEP_LENGTH * value
+        out.append(pltpu.make_async_copy(grad.at[f], grad_hbm.at[0, f], sems.at[1 + 2 * f]))
+        out.append(pltpu.make_async_copy(ana.at[f], ana_hbm.at[0, f], sems.at[2 + 2 * f]))
+        out[-2].start()
+        out[-1].start()
     for copy in out:
         copy.wait()
 
@@ -355,11 +358,11 @@
     hbm = pl.BlockSpec(memory_space=pl.ANY)
     out = jax.ShapeDtypeStruct(start_states.shape, f32)
     dma = pltpu.SemaphoreType.DMA
-    return pl.pallas_call(
+    gradient = pl.pallas_call(
         functools.partial(kernel, n_win, n_strip),
-        out_shape=(out, out),
+        out_shape=pltpu.VMEM((fields, rows * SUBS, LANES), f32),
         in_specs=[hbm] * 5,
-        out_specs=(hbm, hbm),
+        out_specs=pl.BlockSpec(memory_space=pltpu.VMEM),
         scratch_shapes=[
             pltpu.VMEM((fields, rows, cols), f32),
             pltpu.VMEM((fields, SUBS, cols), f32),
@@ -382,15 +385,19 @@
             pltpu.VMEM((fields, steps * SUBS, LANES), f32),
             pltpu.VMEM((fields, steps * SUBS, LANES), f32),
             pltpu.VMEM((fields, steps * SUBS, LANES), f32),
-            pltpu.VMEM((fields, rows, cols), f32),
-            pltpu.VMEM((fields, rows, cols), f32),
             dma((5,)),
-            dma((2,)),
             dma((8,)),
             dma((8,)),
         ],
         compiler_params=pltpu.CompilerParams(collective_id=0, has_side_effects=True),
     )(start_states, obs_cells, obs_values, weighting, live_windows)
+    return pl.pallas_call(
+        finish,
+        out_shape=(out, out),
+        in_specs=[pl.BlockSpec(memory_space=pltpu.VMEM), hbm],
+        out_specs=(hbm, hbm),
+        scratch_shapes=[pltpu.VMEM((fields, rows, cols), f32)] * 3 + [dma((1 + 2 * fields,))],
+    )(pltpu.with_memory_space_constraint(gradient, pltpu.VMEM), start_states)
 
 
 def solution(mesh):

time: 19.2 us -> 17.8 us (0.927)
  the two profiles are of different devices: /device:TPU:21 before, /device:TPU:13 now
where the time goes in v2:
time: 17.8 us; the launch traced here: 17.7 us
  Pallas kernels  16.4 us (92%)
  between operations  1.29 us (7%)
    pallas_call x1, Pallas kernels, per_device(): pl.pallas_call(functools.partial(kernel, n_win, n_strip), out_shape=pltpu...  14.6 us
    pallas_call x1, Pallas kernels, per_device(): pl.pallas_call(finish, out_shape=(out, out), in_specs=[pl.BlockSpec(memor...  1.74 us

profile of v2, /device:TPU:13, one launch (start us, length us, event | category | flops | bytes accessed | tf_op | source)
XLA Modules:
  0.0 17.7 jit_solution(10368184761111623988)
XLA Ops:
  1.3 14.6 %shard_map.68.tiled = f32[3,128,128]{2,1,0:T(8,128)S(1)} custom-call(f32[1,3,16,1024]{3,2,1,0:T(8,128)} %start_hbm.3, s32[1,4,256]{2,1,0:T(4,128)} %cells_hbm.1, f32[1,4,256]{2,1,0:T(4,128)} %values_hbm.1, f32[3,128,128]{2,1,0:T(8,128)} %weight_hbm.1, s32[1]{0:T(128)S(6)} %copy.7.live_hbm), custom_call_target="tpu_custom_call" | custom-call | tf_op jit(solution)/shard_map/pallas_call | solution.py:361
  15.9 1.7 %shard_map.69 = (f32[1,3,16,1024]{3,2,1,0:T(8,128)}, f32[1,3,16,1024]{3,2,1,0:T(8,128)}) custom-call(f32[3,128,128]{2,1,0:T(8,128)S(1)} %shard_map.68.tiled, f32[1,3,16,1024]{3,2,1,0:T(8,128)} %start_hbm.3), custom_call_target="tpu_custom_call" | custom-call | tf_op jit(solution)/shard_map/pallas_call | solution.py:394

commit v3 on v2

--- a/solution.py
+++ b/solution.py
@@ -29,8 +29,8 @@
 def kernel(
     n_win, n_strip,
     start_hbm, cells_hbm, values_hbm, weight_hbm, live_hbm,
-    grad,
-    own, above, below, nxt, prev_end, cells, values, weight, live,
+    grad, own,
+    above, below, nxt, prev_end, cells, values, weight, live,
     rhs, traj, saved, end, lam, counts, sums, nw, spill_up, spill_down, got_top, got_bot,
     local_sem, send_sem, recv_sem,
 ):
@@ -55,14 +55,14 @@
         pltpu.make_async_copy(weight_hbm, weight, local_sem.at[3]),
         pltpu.make_async_copy(live_hbm, live, local_sem.at[4]),
     ]
-    for load in loads:
-        load.start()
-
     barrier = pltpu.get_barrier_semaphore()
     for there, peer in ((has_up, at_strip(-1)), (has_down, at_strip(1)), (has_prev, at_win(-1)), (has_next, at_win(1))):
         @pl.when(there)
         def _():
             pl.semaphore_signal(barrier, inc=1, device_id=peer, device_id_type=pl.DeviceIdType.MESH)
+    for load in loads:
+        load.start()
+
     pl.semaphore_wait(barrier, sum(there.astype(jnp.int32) for there in (has_up, has_down, has_prev, has_next)))
 
     def remote(src, dst, sem, peer):
@@ -74,22 +74,22 @@
     halo_up = remote(start_hbm.at[0, :, 0:SUBS, :], below, 0, at_strip(-1))
     halo_down = remote(start_hbm.at[0, :, rows - SUBS:rows, :], above, 1, at_strip(1))
     start_back = [remote(start_hbm.at[0, f], nxt.at[f], 2 + f, at_win(-1)) for f in range(fields)]
-    end_on = remote(end, prev_end, 5, at_win(1))
-    spill_to_up = remote(spill_up, got_bot, 6, at_strip(-1))
-    spill_to_down = remote(spill_down, got_top, 7, at_strip(1))
-
-    @pl.when(has_up)
-    def _():
-        halo_up.start()
-
-    @pl.when(has_down)
-    def _():
-        halo_down.start()
+    end_on = [remote(end.at[f], prev_end.at[f], 2 + fields + f, at_win(1)) for f in range(fields)]
+    spill_to_up = remote(spill_up, got_bot, 2 + 2 * fields, at_strip(-1))
+    spill_to_down = remote(spill_down, got_top, 3 + 2 * fields, at_strip(1))
 
     @pl.when(has_prev)
     def _():
         for copy in start_back:
             copy.start()
+
+    @pl.when(has_up)
+    def _():
+        halo_up.start()
+
+    @pl.when(has_down)
+    def _():
+        halo_down.start()
 
     lane = lax.broadcasted_iota(jnp.int32, (1, SUBS, LANES), 2)
     first_lane, last_lane = lane == 0, lane == LANES - 1
@@ -221,14 +221,13 @@
                 else:
                     put(end, (f,), lo - steps - pad, x)
 
-    @pl.when(has_next)
-    def _():
-        end_on.start()
-
     for f in range(fields):
         @pl.when(has_next)
         def _():
             start_back[f].wait_recv()
+            if f == 0:
+                for copy in end_on:
+                    copy.start()
             for g in range(0, rows, SUBS):
                 for b in range(SUBS):
                     nw[f, pl.ds(SUBS * g + b, SUBS, stride=SUBS), :] = nxt[f, g:g + SUBS, b * LANES:(b + 1) * LANES]
@@ -290,15 +289,15 @@
 
     last = steps % 2
 
-    @pl.when(has_prev)
-    def _():
-        end_on.wait_recv()
-
-    @pl.when(jnp.logical_not(has_prev))
-    def _():
-        prev_end[...] = jnp.zeros_like(prev_end)
-
-    for f in range(fields):
+    for f in range(fields):
+        @pl.when(has_prev)
+        def _():
+            end_on[f].wait_recv()
+
+        @pl.when(jnp.logical_not(has_prev))
+        def _():
+            prev_end[f] = jnp.zeros((tiles, LANES), jnp.float32)
+
         start = traj[0, f, own_rows, :]
         grad[f] = lam[last, f, own_rows, :] + weigh(f, start - prev_end[f])
 
@@ -320,7 +319,7 @@
         (has_up, [halo_up, spill_to_up]),
         (has_down, [halo_down, spill_to_down]),
         (has_prev, start_back),
-        (has_next, [end_on]),
+        (has_next, end_on),
     ):
         @pl.when(there)
         def _():
@@ -328,11 +327,8 @@
                 copy.wait_send()
 
 
-def finish(tiled, start_hbm, grad_hbm, ana_hbm, own, grad, ana, sems):
+def finish(tiled, own, grad_hbm, ana_hbm, grad, ana, sems):
     fields, rows, _ = own.shape
-    load = pltpu.make_async_copy(start_hbm.at[0], own, sems.at[0])
-    load.start()
-    load.wait()
     out = []
     for f in range(fields):
         for g in range(0, rows, SUBS):
@@ -341,8 +337,8 @@
                 where = (f, slice(g, g + SUBS), slice(b * LANES, (b + 1) * LANES))
                 grad[where] = value
                 ana[where] = own[where] - STEP_LENGTH * value
-        out.append(pltpu.make_async_copy(grad.at[f], grad_hbm.at[0, f], sems.at[1 + 2 * f]))
-        out.append(pltpu.make_async_copy(ana.at[f], ana_hbm.at[0, f], sems.at[2 + 2 * f]))
+        out.append(pltpu.make_async_copy(grad.at[f], grad_hbm.at[0, f], sems.at[2 * f]))
+        out.append(pltpu.make_async_copy(ana.at[f], ana_hbm.at[0, f], sems.at[2 * f + 1]))
         out[-2].start()
         out[-1].start()
     for copy in out:
@@ -358,13 +354,12 @@
     hbm = pl.BlockSpec(memory_space=pl.ANY)
     out = jax.ShapeDtypeStruct(start_states.shape, f32)
     dma = pltpu.SemaphoreType.DMA
-    gradient = pl.pallas_call(
+    tiled, own = pl.pallas_call(
         functools.partial(kernel, n_win, n_strip),
-        out_shape=pltpu.VMEM((fields, rows * SUBS, LANES), f32),
-        in_specs=[hbm] * 5,
-        out_specs=pl.BlockSpec(memory_space=pltpu.VMEM),
+        out_shape=(pltpu.VMEM((fields, rows * SUBS, LANES), f32), pltpu.VMEM((fields, rows, cols), f32)),
+        in_specs=[hbm] * 4 + [pl.BlockSpec(memory_space=pltpu.HBM)],
+        out_specs=(pl.BlockSpec(memory_space=pltpu.VMEM),) * 2,
         scratch_shapes=[
-            pltpu.VMEM((fields, rows, cols), f32),
             pltpu.VMEM((fields, SUBS, cols), f32),
             pltpu.VMEM((fields, SUBS, cols), f32),
             pltpu.VMEM((fields, rows, cols), f32),
@@ -386,18 +381,18 @@
             pltpu.VMEM((fields, steps * SUBS, LANES), f32),
             pltpu.VMEM((fields, steps * SUBS, LANES), f32),
             dma((5,)),
-            dma((8,)),
-            dma((8,)),
+            dma((4 + 2 * fields,)),
+            dma((4 + 2 * fields,)),
         ],
         compiler_params=pltpu.CompilerParams(collective_id=0, has_side_effects=True),
     )(start_states, obs_cells, obs_values, weighting, live_windows)
     return pl.pallas_call(
         finish,
         out_shape=(out, out),
-        in_specs=[pl.BlockSpec(memory_space=pltpu.VMEM), hbm],
+        in_specs=[pl.BlockSpec(memory_space=pltpu.VMEM)] * 2,
         out_specs=(hbm, hbm),
-        scratch_shapes=[pltpu.VMEM((fields, rows, cols), f32)] * 3 + [dma((1 + 2 * fields,))],
-    )(pltpu.with_memory_space_constraint(gradient, pltpu.VMEM), start_states)
+        scratch_shapes=[pltpu.VMEM((fields, rows, cols), f32)] * 2 + [dma((2 * fields,))],
+    )(*(pltpu.with_memory_space_constraint(x, pltpu.VMEM) for x in (tiled, own)))
 
 
 def solution(mesh):

time: 17.8 us -> 15.9 us (0.89)
  the two profiles are of different devices: /device:TPU:13 before, /device:TPU:0 now
where the time goes in v3:
time: 15.9 us; the launch traced here: 15.8 us
  Pallas kernels  14.5 us (91%)
  between operations  1.29 us (8%)
    pallas_call x1, Pallas kernels, per_device(): pl.pallas_call(functools.partial(kernel, n_win, n_strip), out_shape=(pltp...  13.7 us
    pallas_call x1, Pallas kernels, per_device(): pl.pallas_call(finish, out_shape=(out, out), in_specs=[pl.BlockSpec(memor...  0.8 us

profile of v3, /device:TPU:0, one launch (start us, length us, event | category | flops | bytes accessed | tf_op | source)
XLA Modules:
  0.0 15.8 jit_solution(5658575879735998870)
XLA Ops:
  1.3 13.7 %shard_map.68 = (f32[3,128,128]{2,1,0:T(8,128)S(1)}, f32[3,16,1024]{2,1,0:T(8,128)S(1)}) custom-call(f32[1,3,16,1024]{3,2,1,0:T(8,128)} %start_hbm.1, s32[1,4,256]{2,1,0:T(4,128)} %cells_hbm.1, f32[1,4,256]{2,1,0:T(4,128)} %values_hbm.1, f32[3,128,128]{2,1,0:T(8,128)} %weight_hbm.1, s32[1]{0:T(128)S(6)} %copy.7.live_hbm), custom_call_target="tpu_custom_call" | custom-call | tf_op jit(solution)/shard_map/pallas_call | solution.py:357
  14.9 0.8 %shard_map.69 = (f32[1,3,16,1024]{3,2,1,0:T(8,128)}, f32[1,3,16,1024]{3,2,1,0:T(8,128)}) custom-call(f32[3,128,128]{2,1,0:T(8,128)S(1)} %get-tuple-element.4.tiled, f32[3,16,1024]{2,1,0:T(8,128)S(1)} %get-tuple-element.5.own), custom_call_target="tpu_custom_call" | custom-call | tf_op jit(solution)/shard_map/pallas_call | solution.py:389

commit v4 on v3

--- a/solution.py
+++ b/solution.py
@@ -225,9 +225,11 @@
         @pl.when(has_next)
         def _():
             start_back[f].wait_recv()
-            if f == 0:
-                for copy in end_on:
-                    copy.start()
+            if f < 2:
+                @pl.when(win % 2 == 1 - f)
+                def _():
+                    for copy in end_on:
+                        copy.start()
             for g in range(0, rows, SUBS):
                 for b in range(SUBS):
                     nw[f, pl.ds(SUBS * g + b, SUBS, stride=SUBS), :] = nxt[f, g:g + SUBS, b * LANES:(b + 1) * LANES]
@@ -289,31 +291,31 @@
 
     last = steps % 2
 
-    for f in range(fields):
-        @pl.when(has_prev)
-        def _():
-            end_on[f].wait_recv()
-
-        @pl.when(jnp.logical_not(has_prev))
-        def _():
-            prev_end[f] = jnp.zeros((tiles, LANES), jnp.float32)
-
-        start = traj[0, f, own_rows, :]
-        grad[f] = lam[last, f, own_rows, :] + weigh(f, start - prev_end[f])
-
     @pl.when(has_up)
     def _():
         spill_to_down.wait_recv()
         for f in range(fields):
-            at = slice(0, SUBS * steps)
-            grad[f, at, :] = grad[f, at, :] + got_top[f]
+            at = slice(SUBS * (steps + pad), SUBS * (2 * steps + pad))
+            lam[last, f, at, :] = lam[last, f, at, :] + got_top[f]
 
     @pl.when(has_down)
     def _():
         spill_to_up.wait_recv()
         for f in range(fields):
-            at = slice(SUBS * (rows - steps), SUBS * rows)
-            grad[f, at, :] = grad[f, at, :] + got_bot[f]
+            at = slice(SUBS * (rows + pad), SUBS * (steps + rows + pad))
+            lam[last, f, at, :] = lam[last, f, at, :] + got_bot[f]
+
+    for f in range(fields):
+        @pl.when(has_prev)
+        def _():
+            end_on[f].wait_recv()
+
+        @pl.when(jnp.logical_not(has_prev))
+        def _():
+            prev_end[f] = jnp.zeros((tiles, LANES), jnp.float32)
+
+        start = traj[0, f, own_rows, :]
+        grad[f] = lam[last, f, own_rows, :] + weigh(f, start - prev_end[f])
 
     for there, copies in (
         (has_up, [halo_up, spill_to_up]),

time: 15.9 us -> 15.9 us (level)
  no operation moved by 1% of the time
where the time goes in v4:
time: 15.9 us; the launch traced here: 15.8 us
  Pallas kernels  14.5 us (91%)
  between operations  1.29 us (8%)
    pallas_call x1, Pallas kernels, per_device(): pl.pallas_call(functools.partial(kernel, n_win, n_strip), out_shape=(pltp...  13.7 us
    pallas_call x1, Pallas kernels, per_device(): pl.pallas_call(finish, out_shape=(out, out), in_specs=[pl.BlockSpec(memor...  0.8 us

profile of v4, /device:TPU:0, one launch (start us, length us, event | category | flops | bytes accessed | tf_op | source)
XLA Modules:
  0.0 15.8 jit_solution(4608121080036645149)
XLA Ops:
  1.3 13.7 %shard_map.68 = (f32[3,128,128]{2,1,0:T(8,128)S(1)}, f32[3,16,1024]{2,1,0:T(8,128)S(1)}) custom-call(f32[1,3,16,1024]{3,2,1,0:T(8,128)} %start_hbm.1, s32[1,4,256]{2,1,0:T(4,128)} %cells_hbm.1, f32[1,4,256]{2,1,0:T(4,128)} %values_hbm.1, f32[3,128,128]{2,1,0:T(8,128)} %weight_hbm.1, s32[1]{0:T(128)S(6)} %copy.7.live_hbm), custom_call_target="tpu_custom_call" | custom-call | tf_op jit(solution)/shard_map/pallas_call | solution.py:359
  14.9 0.8 %shard_map.69 = (f32[1,3,16,1024]{3,2,1,0:T(8,128)}, f32[1,3,16,1024]{3,2,1,0:T(8,128)}) custom-call(f32[3,128,128]{2,1,0:T(8,128)S(1)} %get-tuple-element.4.tiled, f32[3,16,1024]{2,1,0:T(8,128)S(1)} %get-tuple-element.5.own), custom_call_target="tpu_custom_call" | custom-call | tf_op jit(solution)/shard_map/pallas_call | solution.py:391
